TPU v7x, 128 devices: a whole 4x4x4 slice. The times are simulated.
128 devices in a mesh: dp: 8 (over y, core), mp: 16 (over x, z).
Axes of the slice: x: 4, y: 4, z: 4, core: 2. Of those that a mesh axis runs over, the one named last changes fastest.
Arguments:
- span_tokens: bfloat16 [128, 256, 2560], P(('dp', 'mp')), may hold values from -6 to 6
- decode_tokens: bfloat16 [256, 2560], P(('dp', 'mp')), may hold values from -6 to 6
- norm_gain: float32 [2560], replicated, may hold values from 0.5 to 1.5
- query_weight: bfloat16 [2560, 2560], P(('dp', 'mp')), may hold values from -0.125 to 0.125
- keyval_weight: bfloat16 [2560, 512], P(('dp', 'mp')), may hold values from -0.125 to 0.125
- output_weight: bfloat16 [2560, 2560], P(('dp', 'mp')), may hold values from -0.125 to 0.125
- span_cache: bfloat16 [128, 2048, 512], P(('dp', 'mp')), may hold values from -360 to 360
- decode_cache: bfloat16 [256, 2048, 512], P(('dp', 'mp')), may hold values from -360 to 360
- span_index: int32 [128], P(('dp', 'mp')), may hold values from 0 to 15
- decode_length: int32 [256], P(('dp', 'mp')), may hold values from 1 to 32768
- cache_slot: int32 [256], replicated, may hold values from 0 to 255, each once
Outputs:
- span_output: bfloat16 [128, 256, 2560], P(('dp', 'mp'))
- span_keyval: bfloat16 [128, 256, 512], P(('dp', 'mp'))
- decode_output: bfloat16 [256, 2560], P(('dp', 'mp'))
- decode_keyval: bfloat16 [256, 512], P(('dp', 'mp'))
Inputs may be any that keep to these rules, and one draw needn't show every extreme that they name: `cache_slot`: each cache slot belongs to exactly one request.
All inputs are finite; a program needn't handle non-finite values.
Results may differ from a plain program's by a relative error of at most 0.024.
Values may be sent and summed in bfloat16 or wider, within the bound.
No kernel may reach another device: no remote copies, remote signals or barrier semaphores. Data moves between devices by JAX's collectives and lax.ppermute only.
A program may use at most 128 MiB of HBM per device.

v0:
```python
import jax
import jax.numpy as jnp
from jax import lax
from jax.sharding import PartitionSpec as P


def rms_normed(rows_in, norm_gain):
    widened = rows_in.astype(jnp.float32)
    spread = jnp.mean(widened * widened, axis=-1, keepdims=True)
    return (widened * lax.rsqrt(spread + 1e-06) * norm_gain).astype(jnp.bfloat16)


def rotate(values, positions):
    quarter = values.shape[-1] // 4
    frequency = 10000.0 ** (-jnp.arange(quarter, dtype=jnp.float32) / quarter)
    angles = positions.astype(jnp.float32)[..., None] * frequency
    cos_part = jnp.cos(angles)
    sin_part = jnp.sin(angles)
    first_half = values[..., :quarter]
    second_half = values[..., quarter : 2 * quarter]
    return jnp.concatenate(
        [
            first_half * cos_part - second_half * sin_part,
            second_half * cos_part + first_half * sin_part,
            values[..., 2 * quarter :],
        ],
        -1,
    )


def span_attend(queries, keyval, stored, offset):
    head_dim = queries.shape[-1]
    length = queries.shape[0]
    window = stored.shape[0]
    key_rows = jnp.concatenate([stored[:, :head_dim], keyval[:, :head_dim]], 0)
    value_rows = jnp.concatenate([stored[:, head_dim:], keyval[:, head_dim:]], 0)
    row_ids = jnp.arange(length, dtype=jnp.int32)
    slot_ids = jnp.arange(window, dtype=jnp.int32)
    held_pos = offset - 1 - jnp.mod(offset - 1 - slot_ids, window)
    cache_ok = (held_pos[None, :] >= 0) & (
        held_pos[None, :] >= offset + row_ids[:, None] - window + 1
    )
    own_ok = row_ids[None, :] <= row_ids[:, None]
    allowed = jnp.concatenate([cache_ok, own_ok], 1)

    def one_head(head_queries):
        scores = jnp.dot(
            head_queries, key_rows.T, preferred_element_type=jnp.float32
        ) * head_dim ** (-0.5)
        highest = jnp.max(jnp.where(allowed, scores, -1e30), -1, keepdims=True)
        exp_terms = jnp.where(allowed, jnp.exp(scores - highest), 0.0)
        weights = (exp_terms / jnp.sum(exp_terms, -1, keepdims=True)).astype(jnp.bfloat16)
        return jnp.dot(weights, value_rows, preferred_element_type=jnp.float32).astype(jnp.bfloat16)

    per_head = lax.map(one_head, jnp.transpose(queries, (1, 0, 2)))
    return jnp.transpose(per_head, (1, 0, 2)).reshape(length, -1)


def decode_attend(queries, keyval, stored, length):
    head_dim = queries.shape[-1]
    window = stored.shape[1]
    score_scale = head_dim ** (-0.5)
    exp_scores = (
        jnp.einsum(
            "ehd,ewd->ehw", queries, stored[..., :head_dim], preferred_element_type=jnp.float32
        )
        * score_scale
    )
    self_scores = (
        jnp.einsum("ehd,ed->eh", queries, keyval[:, :head_dim], preferred_element_type=jnp.float32)
        * score_scale
    )
    slot_ids = jnp.arange(window, dtype=jnp.int32)
    allowed = (slot_ids[None, :] < length[:, None]) & (
        slot_ids[None, :] != jnp.mod(length, window)[:, None]
    )
    allowed = allowed[:, None, :]
    highest = jnp.maximum(jnp.max(jnp.where(allowed, exp_scores, -1e30), -1), self_scores)
    exp_cache = jnp.where(allowed, jnp.exp(exp_scores - highest[..., None]), 0.0)
    exp_self = jnp.exp(self_scores - highest)
    denominator = jnp.sum(exp_cache, -1) + exp_self
    weight_cache = (exp_cache / denominator[..., None]).astype(jnp.bfloat16)
    weight_self = (exp_self / denominator).astype(jnp.bfloat16)
    attended = jnp.einsum(
        "ehw,ewd->ehd", weight_cache, stored[..., head_dim:], preferred_element_type=jnp.float32
    )
    attended = attended + weight_self.astype(jnp.float32)[..., None] * keyval[
        :, None, head_dim:
    ].astype(jnp.float32)
    return attended.astype(jnp.bfloat16).reshape(queries.shape[0], -1)


def shards(
    span_tokens,
    decode_tokens,
    norm_gain,
    query_weight,
    keyval_weight,
    output_weight,
    span_cache,
    decode_cache,
    span_index,
    decode_length,
    cache_slot,
):
    span_len = span_tokens.shape[1]
    own_slots = decode_cache.shape[0]
    requests = cache_slot.shape[0]
    head_dim = keyval_weight.shape[1] // 2
    device = lax.axis_index(("dp", "mp"))
    arrived, arrived_len = (
        lax.all_gather(decode_tokens, ("dp", "mp"), axis=0, tiled=True),
        lax.all_gather(decode_length, ("dp", "mp"), axis=0, tiled=True),
    )
    slot_ids = device * own_slots + jnp.arange(own_slots, dtype=jnp.int32)
    picker = cache_slot[None, :] == slot_ids[:, None]
    own_tokens = jnp.dot(
        picker.astype(jnp.bfloat16), arrived, preferred_element_type=jnp.float32
    ).astype(jnp.bfloat16)
    own_length = jnp.sum(jnp.where(picker, arrived_len[None, :], 0), axis=1).astype(jnp.int32)
    offset = span_index[0] * span_len
    positions = jnp.concatenate([offset + jnp.arange(span_len, dtype=jnp.int32), own_length])
    rows_all = jnp.concatenate([span_tokens[0], own_tokens], 0)
    normed = rms_normed(rows_all, norm_gain)
    row_count = rows_all.shape[0]
    columns = normed
    query_all = jnp.dot(
        columns,
        lax.all_gather(query_weight, ("dp", "mp"), axis=0, tiled=True),
        preferred_element_type=jnp.float32,
    )
    keyval_all = jnp.dot(
        columns,
        lax.all_gather(keyval_weight, ("dp", "mp"), axis=0, tiled=True),
        preferred_element_type=jnp.float32,
    )
    queries = rotate(query_all.reshape(row_count, -1, head_dim), positions[:, None]).astype(
        jnp.bfloat16
    )
    key_rows = rotate(keyval_all[:, :head_dim], positions).astype(jnp.bfloat16)
    keyval = jnp.concatenate([key_rows, keyval_all[:, head_dim:].astype(jnp.bfloat16)], 1)
    span_mixed = span_attend(queries[:span_len], keyval[:span_len], span_cache[0], offset)
    decode_mixed = decode_attend(queries[span_len:], keyval[span_len:], decode_cache, own_length)
    attended = jnp.concatenate([span_mixed, decode_mixed], 0)
    columns = attended
    projected = jnp.dot(
        columns,
        lax.all_gather(output_weight, ("dp", "mp"), axis=0, tiled=True),
        preferred_element_type=jnp.float32,
    )
    finished = (rows_all.astype(jnp.float32) + projected).astype(jnp.bfloat16)
    span_output = finished[:span_len][None]
    span_keyval = keyval[:span_len][None]
    served = finished[span_len:]
    decode_keyval = keyval[span_len:]
    everything = lax.all_gather(served, ("dp", "mp"), axis=0, tiled=True)
    arriving_slots = lax.dynamic_slice_in_dim(cache_slot, device * own_slots, own_slots)
    chooser = arriving_slots[:, None] == jnp.arange(requests, dtype=jnp.int32)[None, :]
    decode_output = jnp.dot(
        chooser.astype(jnp.bfloat16), everything, preferred_element_type=jnp.float32
    ).astype(jnp.bfloat16)
    return (span_output, span_keyval, decode_output, decode_keyval)


def solution(mesh):
    return jax.shard_map(
        shards,
        mesh=mesh,
        in_specs=(
            P(("dp", "mp"), None, None),
            P(("dp", "mp"), None),
            P(),
            P(("dp", "mp"), None),
            P(("dp", "mp"), None),
            P(("dp", "mp"), None),
            P(("dp", "mp"), None, None),
            P(("dp", "mp"), None, None),
            P(("dp", "mp")),
            P(("dp", "mp")),
            P(),
        ),
        out_specs=(
            P(("dp", "mp"), None, None),
            P(("dp", "mp"), None, None),
            P(("dp", "mp"), None),
            P(("dp", "mp"), None),
        ),
        check_vma=False,
    )
```

profile of v0, /device:TPU:1, one launch (start us, length us, event | category | flops | bytes accessed | tf_op | source)
XLA Modules:
  0.0 406.3 jit_solution(6080341818031185715)
XLA Ops:
  11.5 69.1 %all-reduce = s32[256]{0:T(256)S(1)} all-reduce(s32[256]{0:T(256)S(1)} %dynamic-update-slice), channel_id=1, replica_groups=mesh['dp'=8,'mp'=16] {'dp','mp'}, use_global_device_ids=true, to_apply=%add | all-reduce | flops 256 | bytes 2048
  82.2 2.7 fusion.54
  84.8 3.2 reshape.227
  89.7 55.2 %all-gather.15.cloned.1.call-done = bf16[128,20,512]{2,1,0:T(8,128)(2,1)} async-done(((bf16[1,20,512]{2,1,0:T(8,128)(2,1)}), bf16[128,20,512]{2,1,0:T(8,128)(2,1)}) %all-gather.15.cloned.1.call-update) | async-done | bytes 2621456 | tf_op jit(solution)/shard_map/all_gather | solution.py:134
  144.9 5.2 %reshape.231 = bf16[2560,512]{1,0:T(8,128)(2,1)} reshape(bf16[128,20,512]{2,1,0:T(8,128)(2,1)} %all-gather.15.cloned.1.call-done) | data formatting | bytes 5242880
  150.1 2.7 fusion.55
  152.9 1.3 subtract_convert_fusion.1
  154.4 1.2 pad_maximum_fusion.2
  155.6 68.3 %all-gather.13.cloned.1.call-done = bf16[128,20,2560]{2,1,0:T(8,128)(2,1)} async-done(((bf16[1,20,2560]{2,1,0:T(8,128)(2,1)}), bf16[128,20,2560]{2,1,0:T(8,128)(2,1)}) %all-gather.13.cloned.1.call-update) | async-done | bytes 13107216 | tf_op jit(solution)/shard_map/all_gather | solution.py:129
  223.8 18.0 %reshape.229 = bf16[2560,2560]{1,0:T(8,128)(2,1)} reshape(bf16[128,20,2560]{2,1,0:T(8,128)(2,1)} %all-gather.13.cloned.1.call-done) | data formatting | bytes 26214400
  241.8 8.5 %fusion.52 = f32[258,2560]{1,0:T(8,128)} fusion(bf16[2560,2560]{1,0:T(8,128)(2,1)} %reshape.229, f32[2560]{0:T(1024)S(1)} %copy-done.12, f32[258]{0:T(512)S(1)} %add_rsqrt_fusion, bf16[2,2560]{1,0:T(2,128)(2,1)S(1)} %convolution_convert_fusion.1, bf16[256,2560]{1,0:T(8,128)(2,1)S(1)} %bitcast.48), kind=kOutput, calls=%fused_computation.102 | convolution fusion | flops 3386280960 | bytes 17081352 | tf_op jit(solution)/shard_map/dot_general | solution.py:127
  250.3 4.5 %reshape.221 = f32[258,10,256]{2,1,0:T(8,128)} reshape(f32[258,2560]{1,0:T(8,128)} %fusion.52) | data formatting | bytes 5283840 | tf_op jit(solution)/shard_map/reshape | solution.py:137
  254.8 1.8 slice.140
  256.6 3.1 subtract_convert_fusion
  259.7 1.1 maximum_bitcast_fusion
  261.4 1.7 copy-done.6
  264.5 1.2 copy.27
  265.7 35.7 %while.10 = (s32[]{:T(128)}, bf16[10,256,256]{1,2,0:T(8,128)(2,1)}, bf16[10,256,256]{2,1,0:T(8,128)(2,1)S(1)}, bf16[2304,256]{1,0:T(8,128)(2,1)S(1)}, pred[256,2...) while((s32[]{:T(128)}, bf16[10,256,256]{1,2,0:T(8,128)(2,1)}, ...), condition=%wide.region_5.6_spmd, body=%wide.region_2.5_spmd.sunk | while | flops 609943040 | bytes 16717421 | solution.py:55
  301.4 3.2 all-gather.17.cloned.1.call-done
  304.7 18.0 %reshape.233 = bf16[2560,2560]{1,0:T(8,128)(2,1)} reshape(bf16[128,20,2560]{2,1,0:T(8,128)(2,1)} %all-gather.17.cloned.1.call-done) | data formatting | bytes 26214400
  322.6 8.8 %fusion.8 = bf16[258,2560]{1,0:T(8,128)(2,1)S(1)} fusion(bf16[2560,2560]{1,0:T(8,128)(2,1)} %reshape.233, bf16[2,2560]{0,1:T(8,128)(2,1)S(1)} %bitcast.50, bf16[256,2560]{0,1:T(8,128)(2,1)} %bitcast.57, bf16[2,2560]{1,0:T(2,128)(2,1)S(1)} %convolution_convert_fusion.1, bf16[256,2560]{1,0:T(8,128)(2,1)S(1)} %bitcast.49), kind=kOutput, calls=%fused_computation.16 | convolution fusion | flops 3388262400 | bytes 17070080 | tf_op jit(solution)/shard_map/dot_general | solution.py:146
  334.7 1.1 slice_bitcast_fusion
  335.8 59.9 %all-gather.19.cloned.1.call-done = bf16[128,2,2560]{2,1,0:T(2,128)(2,1)} async-done(((bf16[1,2,2560]{2,1,0:T(2,128)(2,1)}), bf16[128,2,2560]{2,1,0:T(2,128)(2,1)}) %all-gather.19.cloned.1.call-update) | async-done | bytes 1310736 | tf_op jit(solution)/shard_map/all_gather | solution.py:156
  395.7 3.2 reshape.235
  (143 shorter events, 48.7 us)
Async XLA Ops:
  7.2 77.7 %all-gather.11.cloned.1.call-start = ((), (), s32[]{:S(2)}) async-start(), calls=%async_computation | async-start | bytes 1320960 | tf_op jit(solution)/shard_map/all_gather | solution.py:112
  7.9 137.0 %all-gather.15.cloned.1.call-start = ((), (), s32[]{:S(2)}) async-start(), calls=%async_computation.2 | async-start | bytes 3170304 | tf_op jit(solution)/shard_map/all_gather | solution.py:134
  8.6 215.2 %all-gather.13.cloned.1.call-start = ((), (), s32[]{:S(2)}) async-start(), calls=%async_computation.1 | async-start | bytes 15851520 | tf_op jit(solution)/shard_map/all_gather | solution.py:129
  9.4 295.3 %all-gather.17.cloned.1.call-start = ((), (), s32[]{:S(2)}) async-start(), calls=%async_computation.3 | async-start | bytes 15851520 | tf_op jit(solution)/shard_map/all_gather | solution.py:148
  10.0 385.7 %all-gather.19.cloned.1.call-start = ((), (), s32[]{:S(2)}) async-start(), calls=%async_computation.4 | async-start | bytes 1320960 | tf_op jit(solution)/shard_map/all_gather | solution.py:156
  84.8 3.2 copy-start.11
  88.0 1.3 copy-start.1
  89.7 60.4 %copy-start.2 = (bf16[1,256,2560]{2,1,0:T(8,128)(2,1)S(1)}, bf16[1,256,2560]{2,1,0:T(8,128)(2,1)}, u32[]{:S(2)}) copy-start(bf16[1,256,2560]{2,1,0:T(8,128)(2,1)} %param.13) | copy-start | bytes 3932164
  89.7 60.4 %copy-start.12 = (f32[2560]{0:T(1024)S(1)}, f32[2560]{0:T(1024)}, u32[]{:S(2)}) copy-start(f32[2560]{0:T(1024)} %param.15) | copy-start | bytes 30724
  152.8 1.6 copy-start.8
  152.8 1.6 copy-start
  155.6 86.3 %copy-start.3 = (bf16[1,256,2560]{2,1,0:T(8,128)(2,1)S(1)}, bf16[1,256,2560]{2,1,0:T(8,128)(2,1)}, u32[]{:S(2)}) copy-start(bf16[1,256,2560]{2,1,0:T(8,128)(2,1)} %param.13) | copy-start | bytes 3932164
  254.8 1.8 copy-start.9
  254.8 1.8 copy-start.10
  260.8 2.3 copy-start.6
  266.4 1.3 copy-start.5
  273.5 1.3 copy-start.5
  277.0 1.6 copy-start.5
  280.9 1.3 copy-start.5
  284.4 1.3 copy-start.5
  287.9 1.3 copy-start.5
  291.5 1.3 copy-start.5
  301.4 21.2 %copy-start.4 = (bf16[1,256,2560]{2,1,0:T(8,128)(2,1)S(1)}, bf16[1,256,2560]{2,1,0:T(8,128)(2,1)}, u32[]{:S(2)}) copy-start(bf16[1,256,2560]{2,1,0:T(8,128)(2,1)} %param.13) | copy-start | bytes 3932164
  301.4 21.2 %copy-start.7 = (bf16[2,10,256]{0,2,1:T(8,128)(2,1)S(1)}, bf16[2,10,256]{0,2,1:T(8,128)(2,1)}, u32[]{:S(2)}) copy-start(bf16[2,10,256]{0,2,1:T(8,128)(2,1)} %copy.27) | copy-start | bytes 30724
  (3 other events, 3.8 us)
Sparse Core Ops, SparseCore 0:
  10.8 67.5 all-gather.10
  81.5 63.4 all-gather.14
  148.0 75.7 all-gather.12
  226.8 77.8 all-gather.16
  332.2 63.3 all-gather.18
where the time goes:
time: 408 us; the launch traced here: 406 us
  waiting for transfers between devices  189 us (46%)
  local copies, waits for them, and re-layouts  78.9 us (19%)
  blocking collectives  69.1 us (17%)
  matrix products  37.4 us (9%)
  other arithmetic  16.6 us (4%)
  between operations  14.7 us (4%)
    unnamed x1, blocking collectives  69.1 us
    all_gather x1, waiting for transfers between devices, shards(): lax.all_gather(query_weight, ('dp', 'mp'), axis=0, tiled=True)  68.3 us
    all_gather x1, waiting for transfers between devices, shards(): everything = lax.all_gather(served, ('dp', 'mp'), axis=0, tiled=True)  59.9 us
    all_gather x1, waiting for transfers between devices, shards(): lax.all_gather(keyval_weight, ('dp', 'mp'), axis=0, tiled=True)  55.2 us
    unnamed x32, local copies, waits for them, and re-layouts  51.7 us
    dot_general x1, matrix products, shards(): jnp.dot(columns, lax.all_gather(output_weight, ('dp', 'mp'), axis=0, tile...  8.85 us
    dot_general x1, matrix products, shards(): jnp.dot(columns, lax.all_gather(query_weight, ('dp', 'mp'), axis=0, tiled...  8.51 us
  transfers between devices with their start and end apart: 5, of which 4 were waited for; matrix products, arithmetic and copies ran while one was open for 23% of the time, Pallas kernels for 0%

commit v1 on v0

--- a/solution.py
+++ b/solution.py
@@ -131,7 +131,12 @@
     )
     keyval_all = jnp.dot(
         columns,
-        lax.all_gather(keyval_weight, ("dp", "mp"), axis=0, tiled=True),
+        jnp.concatenate(
+            lax.all_to_all(
+                jnp.stack([keyval_weight] * lax.axis_size(("dp", "mp"))), ("dp", "mp"), 0, 0
+            ),
+            axis=0,
+        ),
         preferred_element_type=jnp.float32,
     )
     queries = rotate(query_all.reshape(row_count, -1, head_dim), positions[:, None]).astype(

time: 408 us -> 364 us (0.89)
  waiting for transfers between devices: 189 us -> 108 us
  blocking collectives: 69.1 us -> 92.5 us
  starting transfers between devices: 0.19 us -> 12.1 us
    all_gather x1 -> x0, waiting for transfers between devices: 55.2 us -> none  [shards(): lax.all_gather(keyval_weight, ('dp', 'mp'), axis=0, tiled=True)]
    all_gather x1, waiting for transfers between devices: 68.3 us -> 42.3 us  [shards(): lax.all_gather(query_weight, ('dp', 'mp'), axis=0, tiled=True)]
    unnamed x1, blocking collectives: 69.1 us -> 92.5 us
    all_to_all x0 -> x1, starting transfers between devices: none -> 11.9 us  [shards(): lax.all_to_all(jnp.stack([keyval_weight] * lax.axis_size(('dp', 'mp'))),...]
    unnamed x32 -> x33, local copies, waits for them, and re-layouts: 51.7 us -> 45.8 us
    reshape x0 -> x1, local copies, waits for them, and re-layouts: none -> 5.29 us  [shards(): jnp.concatenate(lax.all_to_all(jnp.stack([keyval_weight] * lax.axis_size(...]
  transfers between devices with their start and end apart: 5 -> 5, of which waited for: 4 -> 3; matrix products, arithmetic and copies ran while one was open for 23% -> 26% of each run, Pallas kernels for 0% -> 0%
where the time goes in v1:
time: 364 us; the launch traced here: 362 us
  waiting for transfers between devices  108 us (30%)
  blocking collectives  92.5 us (25%)
  local copies, waits for them, and re-layouts  80.9 us (22%)
  matrix products  37.4 us (10%)
  other arithmetic  16 us (4%)
  between operations  14.7 us (4%)
  starting transfers between devices  12.1 us (3%)
    unnamed x1, blocking collectives  92.5 us
    all_gather x1, waiting for transfers between devices, shards(): everything = lax.all_gather(served, ('dp', 'mp'), axis=0, tiled=True)  59.9 us
    unnamed x33, local copies, waits for them, and re-layouts  45.8 us
    all_gather x1, waiting for transfers between devices, shards(): lax.all_gather(query_weight, ('dp', 'mp'), axis=0, tiled=True)  42.3 us
    all_to_all x1, starting transfers between devices, shards(): lax.all_to_all(jnp.stack([keyval_weight] * lax.axis_size(('dp', 'mp'))),...  11.9 us
    dot_general x1, matrix products, shards(): jnp.dot(columns, lax.all_gather(output_weight, ('dp', 'mp'), axis=0, tile...  8.85 us
    dot_general x1, matrix products, shards(): jnp.dot(columns, lax.all_gather(query_weight, ('dp', 'mp'), axis=0, tiled...  8.51 us
    dot_general x10, matrix products, one_head(): jnp.dot(weights, value_rows, preferred_element_type=jnp.float32)  8.01 us
  transfers between devices with their start and end apart: 5, of which 3 were waited for; matrix products, arithmetic and copies ran while one was open for 26% of the time, Pallas kernels for 0%

profile of v1, /device:TPU:1, one launch (start us, length us, event | category | flops | bytes accessed | tf_op | source)
XLA Modules:
  0.0 361.5 jit_solution(14453306683946297199)
XLA Ops:
  9.4 2.7 stack.2
  12.1 11.9 %all-to-all-start = ((bf16[128,20,512]{2,1,0:T(8,128)(2,1)}), bf16[128,20,512]{2,1,0:T(8,128)(2,1)}, u32[]{:S(2)}, u32[]{:S(2)}) async-start(bf16[128,20,512]{2,1,0:T(8,128)(2,1)} %stack.2), calls=%async_computation | async-start | bytes 6291456 | tf_op jit(solution)/shard_map/all_to_all | solution.py:135
  24.9 92.5 %all-reduce = s32[256]{0:T(256)S(1)} all-reduce(s32[256]{0:T(256)S(1)} %dynamic-update-slice), channel_id=1, replica_groups=mesh['dp'=8,'mp'=16] {'dp','mp'}, use_global_device_ids=true, to_apply=%add | all-reduce | flops 256 | bytes 2048
  118.3 2.7 fusion.54
  121.0 3.2 reshape.233
  125.9 5.3 %reshape.227 = bf16[2560,512]{1,0:T(8,128)(2,1)} reshape(bf16[128,20,512]{2,1,0:T(8,128)(2,1)} %all-to-all-done) | data formatting | bytes 5242880 | tf_op jit(solution)/shard_map/reshape | solution.py:134
  131.2 2.7 fusion.55
  133.9 1.3 subtract_convert_fusion.1
  135.5 1.2 pad_maximum_fusion.2
  136.6 42.3 %all-gather.11.cloned.1.call-done = bf16[128,20,2560]{2,1,0:T(8,128)(2,1)} async-done(((bf16[1,20,2560]{2,1,0:T(8,128)(2,1)}), bf16[128,20,2560]{2,1,0:T(8,128)(2,1)}) %all-gather.11.cloned.1.call-update) | async-done | bytes 13107216 | tf_op jit(solution)/shard_map/all_gather | solution.py:129
  178.9 18.0 %reshape.235 = bf16[2560,2560]{1,0:T(8,128)(2,1)} reshape(bf16[128,20,2560]{2,1,0:T(8,128)(2,1)} %all-gather.11.cloned.1.call-done) | data formatting | bytes 26214400
  196.9 8.5 %fusion.52 = f32[258,2560]{1,0:T(8,128)} fusion(bf16[2560,2560]{1,0:T(8,128)(2,1)} %reshape.235, f32[2560]{0:T(1024)S(1)} %copy-done.12, f32[258]{0:T(512)S(1)} %add_rsqrt_fusion, bf16[2,2560]{1,0:T(2,128)(2,1)S(1)} %convolution_convert_fusion.1, bf16[256,2560]{1,0:T(8,128)(2,1)S(1)} %bitcast.47), kind=kOutput, calls=%fused_computation.102 | convolution fusion | flops 3386280960 | bytes 17081352 | tf_op jit(solution)/shard_map/dot_general | solution.py:127
  205.4 4.5 %reshape.226 = f32[258,10,256]{2,1,0:T(8,128)} reshape(f32[258,2560]{1,0:T(8,128)} %fusion.52) | data formatting | bytes 5283840 | tf_op jit(solution)/shard_map/reshape | solution.py:142
  209.9 1.8 slice.140
  211.7 3.1 subtract_convert_fusion
  216.5 1.6 copy-done.6
  219.6 1.2 copy.27
  220.8 35.6 %while.10 = (s32[]{:T(128)}, bf16[10,256,256]{1,2,0:T(8,128)(2,1)}, bf16[10,256,256]{2,1,0:T(8,128)(2,1)S(1)}, bf16[2304,256]{1,0:T(8,128)(2,1)S(1)}, pred[256,2...) while((s32[]{:T(128)}, bf16[10,256,256]{1,2,0:T(8,128)(2,1)}, ...), condition=%wide.region_5.6_spmd, body=%wide.region_2.5_spmd.sunk | while | flops 609943040 | bytes 16717421 | solution.py:55
  256.4 3.5 all-gather.13.cloned.1.call-done
  259.9 18.0 %reshape.237 = bf16[2560,2560]{1,0:T(8,128)(2,1)} reshape(bf16[128,20,2560]{2,1,0:T(8,128)(2,1)} %all-gather.13.cloned.1.call-done) | data formatting | bytes 26214400
  277.9 8.8 %fusion.8 = bf16[258,2560]{1,0:T(8,128)(2,1)S(1)} fusion(bf16[2560,2560]{1,0:T(8,128)(2,1)} %reshape.237, bf16[2,2560]{0,1:T(8,128)(2,1)S(1)} %bitcast.49, bf16[256,2560]{0,1:T(8,128)(2,1)} %bitcast.55, bf16[2,2560]{1,0:T(2,128)(2,1)S(1)} %convolution_convert_fusion.1, bf16[256,2560]{1,0:T(8,128)(2,1)S(1)} %bitcast.48), kind=kOutput, calls=%fused_computation.16 | convolution fusion | flops 3388262400 | bytes 17070080 | tf_op jit(solution)/shard_map/dot_general | solution.py:151
  289.9 1.1 slice_bitcast_fusion
  291.0 59.9 %all-gather.15.cloned.1.call-done = bf16[128,2,2560]{2,1,0:T(2,128)(2,1)} async-done(((bf16[1,2,2560]{2,1,0:T(2,128)(2,1)}), bf16[128,2,2560]{2,1,0:T(2,128)(2,1)}) %all-gather.15.cloned.1.call-update) | async-done | bytes 1310736 | tf_op jit(solution)/shard_map/all_gather | solution.py:161
  350.9 3.2 reshape.239
  (145 shorter events, 47.8 us)
Async XLA Ops:
  7.2 113.8 %all-gather.9.cloned.1.call-start = ((), (), s32[]{:S(2)}) async-start(), calls=%async_computation.1 | async-start | bytes 1320960 | tf_op jit(solution)/shard_map/all_gather | solution.py:112
  7.9 171.0 %all-gather.11.cloned.1.call-start = ((), (), s32[]{:S(2)}) async-start(), calls=%async_computation.2 | async-start | bytes 15851520 | tf_op jit(solution)/shard_map/all_gather | solution.py:129
  8.6 251.3 %all-gather.13.cloned.1.call-start = ((), (), s32[]{:S(2)}) async-start(), calls=%async_computation.3 | async-start | bytes 15851520 | tf_op jit(solution)/shard_map/all_gather | solution.py:153
  12.1 12.6 %copy-start.13 = (s32[2]{0:T(128)S(1)}, s32[2]{0:T(128)}, u32[]{:S(2)}) copy-start(s32[2]{0:T(128)} %param.22) | copy-start | bytes 28
  12.1 105.4 %copy-start.11 = (s32[256]{0:T(256)S(1)}, s32[256]{0:T(256)}, u32[]{:S(2)}) copy-start(s32[256]{0:T(256)} %param.23) | copy-start | bytes 3076
  12.1 113.8 %all-to-all-start = ((bf16[128,20,512]{2,1,0:T(8,128)(2,1)}), bf16[128,20,512]{2,1,0:T(8,128)(2,1)}, u32[]{:S(2)}, u32[]{:S(2)}) async-start(bf16[128,20,512]{2,1,0:T(8,128)(2,1)} %stack.2), calls=%async_computation | async-start | bytes 6291456 | tf_op jit(solution)/shard_map/all_to_all | solution.py:135
  24.0 326.9 %all-gather.15.cloned.1.call-start = ((), (), s32[]{:S(2)}) async-start(), calls=%async_computation.4 | async-start | bytes 1320960 | tf_op jit(solution)/shard_map/all_gather | solution.py:161
  124.2 1.3 copy-start.1
  125.9 5.3 %copy-start.2 = (bf16[1,256,2560]{2,1,0:T(8,128)(2,1)S(1)}, bf16[1,256,2560]{2,1,0:T(8,128)(2,1)}, u32[]{:S(2)}) copy-start(bf16[1,256,2560]{2,1,0:T(8,128)(2,1)} %param.13) | copy-start | bytes 3932164
  125.9 5.3 %copy-start.12 = (f32[2560]{0:T(1024)S(1)}, f32[2560]{0:T(1024)}, u32[]{:S(2)}) copy-start(f32[2560]{0:T(1024)} %param.15) | copy-start | bytes 30724
  133.9 1.6 copy-start.8
  133.9 1.6 copy-start
  136.6 60.3 %copy-start.3 = (bf16[1,256,2560]{2,1,0:T(8,128)(2,1)S(1)}, bf16[1,256,2560]{2,1,0:T(8,128)(2,1)}, u32[]{:S(2)}) copy-start(bf16[1,256,2560]{2,1,0:T(8,128)(2,1)} %param.13) | copy-start | bytes 3932164
  209.9 1.8 copy-start.9
  209.9 1.8 copy-start.10
  215.9 2.3 copy-start.6
  221.5 1.3 copy-start.5
  228.6 1.3 copy-start.5
  232.1 1.4 copy-start.5
  235.8 1.3 copy-start.5
  239.4 1.3 copy-start.5
  246.5 1.3 copy-start.5
  256.4 21.5 %copy-start.4 = (bf16[1,256,2560]{2,1,0:T(8,128)(2,1)S(1)}, bf16[1,256,2560]{2,1,0:T(8,128)(2,1)}, u32[]{:S(2)}) copy-start(bf16[1,256,2560]{2,1,0:T(8,128)(2,1)} %param.13) | copy-start | bytes 3932164
  256.4 21.5 %copy-start.7 = (bf16[2,10,256]{0,2,1:T(8,128)(2,1)S(1)}, bf16[2,10,256]{0,2,1:T(8,128)(2,1)}, u32[]{:S(2)}) copy-start(bf16[2,10,256]{0,2,1:T(8,128)(2,1)} %copy.27) | copy-start | bytes 30724
  (4 other events, 5.1 us)
Sparse Core Ops, SparseCore 0:
  10.8 88.9 all-gather.8
  102.8 76.0 all-gather.10
  182.0 77.8 all-gather.12
  287.5 63.3 all-gather.14
